TPU v7x, 32 devices: a whole 2x2x4 slice. The times are simulated.
32 devices in a mesh: tile: 4 (over y, core), dp: 8 (over z, x).
Axes of the slice: x: 2, y: 2, z: 4, core: 2. Of those that a mesh axis runs over, the one named last changes fastest.
Arguments:
- observed: float32 [8, 2, 8, 32], P('dp', None, 'tile'), may hold values from -6 to 6
- targets: float32 [8, 2, 8, 32], P('dp', None, 'tile'), may hold values from -6 to 6
- pixel_mask: int32 [8, 2, 8, 32], P('dp', None, 'tile'), may hold values 0 or 1
- lengths: int32 [8], P('dp'), may hold values from 1 to 2, as said below
- step_count: int32 [1], replicated, may hold values from 2 to 20
- kernels: float32 [1, 12800, 1024], P(None, 'dp'), may hold values from -0.0546875 to 0.0546875
- kernel_moment: float32 [1, 12800, 1024], P(None, 'dp'), may hold values from -7.6293945e-06 to 7.6293945e-06
- kernel_second: float32 [1, 12800, 1024], P(None, 'dp'), may hold values from 1.9073486e-12 to 7.6293945e-12
- norm_params: float32 [2, 1, 1024], replicated
- norm_moment: float32 [2, 1, 1024], replicated, may hold values from -1.5258789e-05 to 1.5258789e-05
- norm_second: float32 [2, 1, 1024], replicated, may hold values from 7.6293945e-12 to 3.0517578e-11
- end_params: float32 [3, 256], replicated
- end_moment: float32 [3, 256], replicated, may hold values from -7.6293945e-05 to 7.6293945e-05
- end_second: float32 [3, 256], replicated, may hold values from 1.9073486e-10 to 7.6293943e-10
- head_bias: float32 [1], replicated, may hold values from -3 to 3
- head_moment: float32 [1], replicated, may hold values from -0.0546875 to 0.0546875
- head_second: float32 [1], replicated, may hold values from 7.6293945e-05 to 0.00030517578
- hidden_init: float32 [1, 8, 8, 32, 256], P(None, 'dp', 'tile'), may hold values from -0.9 to 0.9
- cells_init: float32 [1, 8, 8, 32, 256], P(None, 'dp', 'tile'), may hold values from -5 to 5
Outputs:
- loss_value: float32 [], replicated
- grad_norm: float32 [], replicated
- kernels_new: float32 [1, 12800, 1024], P(None, 'dp')
- kernel_moment_new: float32 [1, 12800, 1024], P(None, 'dp')
- kernel_second_new: float32 [1, 12800, 1024], P(None, 'dp')
- norm_new: float32 [2, 1, 1024], replicated
- norm_moment_new: float32 [2, 1, 1024], replicated
- norm_second_new: float32 [2, 1, 1024], replicated
- end_new: float32 [3, 256], replicated
- end_moment_new: float32 [3, 256], replicated
- end_second_new: float32 [3, 256], replicated
- head_new: float32 [1], replicated
- head_moment_new: float32 [1], replicated
- head_second_new: float32 [1], replicated
- hidden_final: float32 [1, 8, 8, 32, 256], P(None, 'dp', 'tile')
- cells_final: float32 [1, 8, 8, 32, 256], P(None, 'dp', 'tile')
Inputs may be any that keep to these rules, and one draw needn't show every extreme that they name: `lengths`: some stream has all 2 frames counting and some only one.
All inputs are finite; a program needn't handle non-finite values. No bound on the sum of `pixel_mask` on one device may be relied on, other than what follows from the above.
Results may differ from a plain program's by a relative error of at most 0.0003.
The roundings to bfloat16 on the way count: a program that leaves them out, or rounds other values in their place, can miss the bound.
Values may be sent and summed in bfloat16 or wider, within the bound.
No kernel may reach another device: no remote copies, remote signals or barrier semaphores. Data moves between devices by JAX's collectives and lax.ppermute only.
A program may use at most 192 MiB of HBM per device.

v0:
```python
import jax
import jax.numpy as jnp
from jax import lax
from jax.sharding import PartitionSpec as P

IN_DIM = 512
KERNEL = 5
GROUP_SIZE = 64
clip_limit = 0.005
small_rate = 0.1


def padded_2(cells, sides, width):
    for axis, dim in sides:
        count = lax.axis_size(axis)
        ends = count - 1
        head = lax.slice_in_dim(cells, 0, width, axis=dim)
        tail = lax.slice_in_dim(cells, cells.shape[dim] - width, cells.shape[dim], axis=dim)
        cells = jnp.concatenate(
            [
                lax.ppermute(tail, axis, [(i, (i + 1) % count) for i in range(ends)]),
                cells,
                lax.ppermute(head, axis, [((i + 1) % count, i) for i in range(ends)]),
            ],
            axis=dim,
        )
    return cells


def group_norm(gates, gain, shift):
    full_shape = gates.shape
    grouped = gates.reshape(full_shape[:-1] + (full_shape[-1] // GROUP_SIZE, GROUP_SIZE))
    centred = grouped - jnp.mean(grouped, axis=-1, keepdims=True)
    spread = jnp.mean(centred * centred, axis=-1, keepdims=True)
    return (centred * lax.rsqrt(spread + 1e-05)).reshape(full_shape) * gain + shift


def lstm_cell(gates, cells_prev, gain, shift):
    normed = group_norm(gates, gain, shift)
    quarter = normed.shape[-1] // 4
    input_gate = jax.nn.sigmoid(normed[..., :quarter])
    forget_gate = jax.nn.sigmoid(normed[..., quarter : 2 * quarter])
    candidate = jnp.tanh(normed[..., 2 * quarter : 3 * quarter])
    output_gate = jax.nn.sigmoid(normed[..., 3 * quarter :])
    cells_next = forget_gate * cells_prev + input_gate * candidate
    return (output_gate * jnp.tanh(cells_next), cells_next)


def unfold(padded, rows, columns):
    pieces = []
    for row_off in range(KERNEL):
        for col_off in range(KERNEL):
            pieces.append(padded[:, row_off : row_off + rows, col_off : col_off + columns, :])
    joined = jnp.concatenate(pieces, axis=-1)
    return joined.reshape(-1, joined.shape[-1])


def pad_columns(values):
    margin = KERNEL // 2
    return jnp.pad(values, ((0, 0), (0, 0), (margin, margin), (0, 0)))


def layer_forward(weight_full, gain, shift, inputs_low, hidden_start, cells_start):
    rows, columns = (hidden_start.shape[1], hidden_start.shape[2])
    hidden_low = hidden_start.astype(jnp.bfloat16)
    cells = cells_start
    kept = []
    outputs = []
    outputs_low = []
    hidden = hidden_start
    for frame_no in range(len(inputs_low)):
        joined = jnp.concatenate([inputs_low[frame_no], hidden_low], axis=-1)
        padded = padded_2(joined, (("tile", 1),), KERNEL // 2)
        padded = pad_columns(padded)
        gates = jnp.dot(
            unfold(padded, rows, columns), weight_full, preferred_element_type=jnp.float32
        )
        gates = gates.reshape(hidden_start.shape[:3] + (weight_full.shape[1],))
        kept.append((padded, gates, cells))
        hidden, cells = lstm_cell(gates, cells, gain, shift)
        hidden_low = hidden.astype(jnp.bfloat16)
        outputs.append(hidden)
        outputs_low.append(hidden_low)
    return (outputs, outputs_low, kept, hidden, cells)


def layer_backward(weight_full, gain, shift, kept, grad_above):
    pixel_shape = kept[0][1].shape
    rows, columns, gate_dim = (pixel_shape[1], pixel_shape[2], pixel_shape[3])
    in_dim = weight_full.shape[0] // (KERNEL * KERNEL)
    half = in_dim // 2
    flipped = weight_full.reshape(KERNEL, KERNEL, in_dim, gate_dim)[::-1, ::-1]
    flipped = flipped.transpose(0, 1, 3, 2).reshape(KERNEL * KERNEL * gate_dim, in_dim)
    grad_weight = jnp.zeros(weight_full.shape, jnp.float32)
    grad_gain = jnp.zeros(gain.shape, jnp.float32)
    grad_shift = jnp.zeros(shift.shape, jnp.float32)
    grad_hidden = jnp.zeros(pixel_shape[:3] + (half,), jnp.float32)
    grad_cells = jnp.zeros(pixel_shape[:3] + (half,), jnp.float32)
    grad_inputs = [None] * len(kept)
    for frame_no in reversed(range(len(kept))):
        padded, gates, cells_prev = kept[frame_no]
        unused, pull = jax.vjp(lstm_cell, gates, cells_prev, gain, shift)
        grad_gates, grad_cells, part_gain, part_shift = pull(
            (grad_above[frame_no] + grad_hidden, grad_cells)
        )
        grad_gain = grad_gain + part_gain
        grad_shift = grad_shift + part_shift
        gates_low = grad_gates.astype(jnp.bfloat16)
        grad_weight = grad_weight + lax.dot_general(
            unfold(padded, rows, columns),
            gates_low.reshape(-1, gate_dim),
            (((0,), (0,)), ((), ())),
            preferred_element_type=jnp.float32,
        )
        spread = padded_2(gates_low, (("tile", 1),), KERNEL // 2)
        spread = pad_columns(spread)
        grad_joined = jnp.dot(
            unfold(spread, rows, columns), flipped, preferred_element_type=jnp.float32
        )
        grad_joined = grad_joined.reshape(pixel_shape[:3] + (in_dim,))
        grad_inputs[frame_no] = grad_joined[..., :half]
        grad_hidden = grad_joined[..., half:]
    return (grad_weight, grad_gain, grad_shift, grad_inputs)


def adamw(weight, moment, second, grad, rate, correction):
    moment_new = 0.5 * moment + 0.5 * grad
    second_new = 0.5 * second + 0.5 * grad * grad
    update = moment_new / correction / (jnp.sqrt(second_new / correction) + 1e-08)
    return (weight - rate * (update + 0.01 * weight), moment_new, second_new)


def per_device(
    observed,
    targets,
    pixel_mask,
    lengths,
    step_count,
    kernels,
    kernel_moment,
    kernel_second,
    norm_params,
    norm_moment,
    norm_second,
    end_params,
    end_moment,
    end_second,
    head_bias,
    head_moment,
    head_second,
    hidden_init,
    cells_init,
):
    frame_total = observed.shape[1]
    layers = kernels.shape[0]
    frame_ids = lax.broadcasted_iota(jnp.int32, (1, frame_total), 1)
    counted = (frame_ids < lengths[:, None]).astype(jnp.float32)
    valid = pixel_mask.astype(jnp.float32) * counted[:, :, None, None]
    count = jnp.maximum(lax.psum(jnp.sum(valid), ("tile", "dp")), 1.0)
    inputs_low = [
        (end_params[0] * observed[:, frame_no, :, :, None] + end_params[1]).astype(jnp.bfloat16)
        for frame_no in range(frame_total)
    ]
    outputs = []
    layer_no = 0
    weight_full = lax.all_gather(kernels[layer_no].astype(jnp.bfloat16), "dp", axis=0, tiled=True)
    outputs, outputs_low, kept, hidden, cells = layer_forward(
        weight_full,
        norm_params[0, layer_no],
        norm_params[1, layer_no],
        inputs_low,
        hidden_init[layer_no],
        cells_init[layer_no],
    )
    stored_kept = [kept]
    hidden_list = [hidden]
    cells_list = [cells]
    loss_sum = jnp.zeros((), jnp.float32)
    grad_head_weight = jnp.zeros(end_params.shape[1:], jnp.float32)
    grad_head = jnp.zeros((1,), jnp.float32)
    grad_above = []
    for frame_no in range(frame_total):
        predicted = jnp.sum(outputs[frame_no] * end_params[2], axis=-1) + head_bias[0]
        error = predicted - targets[:, frame_no]
        weighted = valid[:, frame_no] * error
        loss_sum = loss_sum + jnp.sum(weighted * error)
        grad_pred = 2.0 * weighted / count
        grad_head = grad_head + jnp.sum(grad_pred)
        grad_head_weight = grad_head_weight + jnp.sum(
            grad_pred[..., None] * outputs[frame_no], axis=(0, 1, 2)
        )
        grad_above.append(grad_pred[..., None] * end_params[2])
    kernel_grads = [None] * layers
    gain_grads = [None] * layers
    shift_grads = [None] * layers
    for layer_no in reversed(range(layers)):
        weight_full = lax.all_gather(
            kernels[layer_no].astype(jnp.bfloat16), "dp", axis=0, tiled=True
        )
        grad_weight, grad_gain, grad_shift, grad_inputs = layer_backward(
            weight_full,
            norm_params[0, layer_no],
            norm_params[1, layer_no],
            stored_kept[layer_no],
            grad_above,
        )
        kernel_grads[layer_no] = grad_weight
        gain_grads[layer_no] = grad_gain
        shift_grads[layer_no] = grad_shift
        grad_above = grad_inputs
    grad_lift_weight = jnp.zeros(end_params.shape[1:], jnp.float32)
    grad_lift_bias = jnp.zeros(end_params.shape[1:], jnp.float32)
    for frame_no in range(frame_total):
        grad_lift_weight = grad_lift_weight + jnp.sum(
            grad_above[frame_no] * observed[:, frame_no, :, :, None], axis=(0, 1, 2)
        )
        grad_lift_bias = grad_lift_bias + jnp.sum(grad_above[frame_no], axis=(0, 1, 2))
    grad_norms = jnp.stack([jnp.stack(gain_grads), jnp.stack(shift_grads)])
    grad_ends = jnp.stack([grad_lift_weight, grad_lift_bias, grad_head_weight])
    grad_kernels = jnp.stack(kernel_grads)
    shard = lax.psum_scatter(grad_kernels, "dp", scatter_dimension=1, tiled=True)
    shard = lax.psum(shard, "tile")
    local_square = jnp.sum(shard * shard)
    grad_norms, grad_ends, grad_head, loss_sum = lax.psum(
        (grad_norms, grad_ends, grad_head, loss_sum), ("tile", "dp")
    )
    kernel_square = lax.psum(local_square, "dp")
    squares = (
        kernel_square
        + jnp.sum(grad_norms * grad_norms)
        + jnp.sum(grad_ends * grad_ends)
        + jnp.sum(grad_head * grad_head)
    )
    grad_norm = jnp.sqrt(squares)
    factor = clip_limit / jnp.maximum(grad_norm, clip_limit)
    correction = 1.0 - jnp.power(0.5, step_count[0].astype(jnp.float32))
    kernel_rate = (KERNEL * KERNEL * IN_DIM) ** (-0.5)
    kern_out = adamw(kernels, kernel_moment, kernel_second, shard * factor, kernel_rate, correction)
    norm_out = adamw(
        norm_params, norm_moment, norm_second, grad_norms * factor, small_rate, correction
    )
    end_out = adamw(end_params, end_moment, end_second, grad_ends * factor, small_rate, correction)
    head_out = adamw(
        head_bias, head_moment, head_second, grad_head * factor, small_rate, correction
    )
    loss_value = loss_sum / count
    return (
        loss_value,
        grad_norm,
        kern_out[0],
        kern_out[1],
        kern_out[2],
        norm_out[0],
        norm_out[1],
        norm_out[2],
        end_out[0],
        end_out[1],
        end_out[2],
        head_out[0],
        head_out[1],
        head_out[2],
        jnp.stack(hidden_list),
        jnp.stack(cells_list),
    )


def solution(mesh):
    placed = (
        P("dp", None, "tile", None),
        P("dp", None, "tile", None),
        P("dp", None, "tile", None),
        P("dp"),
        P(),
        P(None, "dp", None),
        P(None, "dp", None),
        P(None, "dp", None),
        P(),
        P(),
        P(),
        P(),
        P(),
        P(),
        P(),
        P(),
        P(),
        P(None, "dp", "tile", None, None),
        P(None, "dp", "tile", None, None),
    )
    return jax.shard_map(
        per_device,
        mesh=mesh,
        in_specs=placed,
        out_specs=(
            P(),
            P(),
            P(None, "dp", None),
            P(None, "dp", None),
            P(None, "dp", None),
            P(),
            P(),
            P(),
            P(),
            P(),
            P(),
            P(),
            P(),
            P(),
            P(None, "dp", "tile", None, None),
            P(None, "dp", "tile", None, None),
        ),
        check_vma=False,
    )
```

profile of v0, /device:TPU:0, one launch (start us, length us, event | category | flops | bytes accessed | tf_op | source)
XLA Modules:
  0.0 1688.5 jit_solution(5633768059832277343)
XLA Ops:
  7.2 5.1 convert_element_type.95
  13.2 1.3 collective-permute-start.1
  14.5 3.0 collective-permute-start
  18.2 0.7 fusion.79
  18.9 85.6 %psum.50 = f32[]{:T(128)} all-reduce(f32[]{:T(128)} %get-tuple-element.65), channel_id=1, replica_groups=mesh['tile'=4,'dp'=8] {'tile','dp'}, use_global_device_ids=true, to_apply=%region_10.11 | all-reduce | flops 1 | bytes 8 | tf_op jit(solution)/shard_map/psum | solution.py:159
  107.0 1.2 copy-done.1
  108.5 408.1 %all-gather.3.cloned.1.call-done = bf16[1,12800,1024]{2,1,0:T(8,128)(2,1)} async-done(((bf16[1,1600,1024]{2,1,0:T(8,128)(2,1)}), bf16[1,12800,1024]{2,1,0:T(8,128)(2,1)}) %all-gather.3.cloned.1.call-update) | async-done | bytes 26214416 | tf_op jit(solution)/shard_map/all_gather | solution.py:166
  516.7 10.8 fusion.3
  529.2 0.8 multiply_add_fusion.2
  530.1 1.3 collective-permute-start.3
  531.4 3.0 collective-permute-start.2
  534.4 18.4 %reverse_bitcast_fusion = bf16[5,5,1024,512]{2,3,1,0:T(8,128)(2,1)} fusion(bf16[5,5,512,1024]{3,2,1,0:T(8,128)(2,1)} %bitcast.214), kind=kLoop, calls=%fused_computation.6 | loop fusion | bytes 52428800 | tf_op jit(solution)/shard_map/transpose | solution.py:93
  552.8 33.9 %copy.35 = bf16[5,5,1024,512]{3,2,1,0:T(8,128)(2,1)} copy(bf16[5,5,1024,512]{2,3,1,0:T(8,128)(2,1)} %reverse_bitcast_fusion) | data formatting | bytes 52428800 | tf_op jit(solution)/shard_map/transpose | solution.py:93
  588.0 0.7 copy-done
  588.8 10.8 fusion.1
  601.3 0.8 multiply_add_fusion.1
  602.0 0.7 fusion.74
  603.6 0.6 fusion.20
  605.0 1.0 fusion.25
  606.1 1.3 collective-permute-start.5
  607.4 3.8 collective-permute-start.4
  611.2 21.6 %fusion.11 = f32[12800,1024,1]{1,0,2:T(8,128)} fusion(bf16[1,2,32,12800]{3,2,1,0:T(8,128)(2,1)} %copy-done, bf16[1,2,32,1024]{3,2,1,0:T(8,128)(2,1)S(1)} %fusion.25), kind=kOutput, calls=%fused_computation.17 | convolution fusion | flops 1677721600 | bytes 54198272 | tf_op jit(solution)/shard_map/dot_general | solution.py:109
  633.8 10.8 fusion.13
  645.5 0.6 fusion.21
  646.9 1.0 fusion.27
  647.9 33.5 %fusion = f32[1,12800,1024]{2,1,0:T(8,128)} fusion(f32[12800,1024,1]{1,0,2:T(8,128)} %fusion.11, bf16[1,2,32,12800]{3,2,1,0:T(8,128)(2,1)S(1)} %copy-done.2, bf16[1,2,32,1024]{3,2,1,0:T(8,128)(2,1)S(1)} %fusion.27), kind=kOutput, calls=%fused_computation.1 | convolution fusion | flops 1690828800 | bytes 106627072 | tf_op jit(solution)/shard_map/dot_general | solution.py:109
  683.5 1.3 collective-permute-start.7
  684.8 4.5 collective-permute-start.6
  689.3 0.6 fusion.72
  692.8 0.7 constant_dynamic-update-slice_fusion.153
  693.4 0.7 constant_dynamic-update-slice_fusion.152
  694.1 0.7 constant_dynamic-update-slice_fusion.151
  694.8 0.7 constant_dynamic-update-slice_fusion.150
  695.5 0.7 constant_dynamic-update-slice_fusion.149
  696.2 0.7 constant_dynamic-update-slice_fusion.148
  696.8 0.7 constant_dynamic-update-slice_fusion.147
  697.5 0.7 constant_dynamic-update-slice_fusion.146
  698.2 0.7 constant_dynamic-update-slice_fusion.145
  698.9 0.7 constant_dynamic-update-slice_fusion.144
  699.6 0.7 constant_dynamic-update-slice_fusion.143
  700.2 0.7 constant_dynamic-update-slice_fusion.142
  700.9 0.7 constant_dynamic-update-slice_fusion.141
  701.6 0.7 constant_dynamic-update-slice_fusion.140
  702.3 0.7 constant_dynamic-update-slice_fusion.139
  703.0 0.7 constant_dynamic-update-slice_fusion.138
  703.6 0.7 constant_dynamic-update-slice_fusion.137
  704.3 0.7 constant_dynamic-update-slice_fusion.136
  705.0 0.7 constant_dynamic-update-slice_fusion.135
  705.7 793.9 %reduce-scatter.2.cloned.1.call-done = f32[1,1600,1024]{2,1,0:T(8,128)} async-done(((f32[1,12800,1024]{2,1,0:T(8,128)}), f32[1,1600,1024]{2,1,0:T(8,128)}) %reduce-scatter.2.cloned.1.call-update) | async-done | bytes 6553616 | tf_op jit(solution)/shard_map/reduce_scatter | solution.py:221
  1499.6 0.7 constant_dynamic-update-slice_fusion.134
  1500.3 0.7 constant_dynamic-update-slice_fusion.133
  1501.0 0.7 constant_dynamic-update-slice_fusion.132
  1501.7 0.7 constant_dynamic-update-slice_fusion.131
  1502.4 0.7 constant_dynamic-update-slice_fusion.130
  1503.0 0.7 constant_dynamic-update-slice_fusion.129
  1503.7 12.9 fusion.16
  1516.8 41.4 %all-reduce.12 = (f32[]{:T(128)}, f32[2,1,1024]{2,1,0:T(1,128)S(1)}, f32[3,256]{1,0:T(4,128)S(1)}, f32[1]{0:T(128)}) all-reduce(f32[]{:T(128)S(6)} %add.410, f32[2,1,1024]{2,1,0:T(1,128)S(1)} %pad_maximum_fusion.14, f32[3,256]{1,0:T(4,128)S(1)} %pad_maximum_fusion.15, f32[1]{0:T(128)} %bitcast.95), channel_id=1, replica_groups=mesh['tile'=4,'dp'=8] {'tile','dp'}, use_global_device_ids=true, to_apply=%region_8.9 | all-reduce | flops 2818 | bytes 22544 | tf_op jit(solution)/shard_map/psum | solution.py:224
  1559.4 0.6 multiply_reduce_fusion.13
  1560.1 66.4 %all-reduce.15.cloned.1.call-done = f32[1,1600,1024]{2,1,0:T(8,128)} async-done(((f32[1,1600,1024]{2,1,0:T(8,128)}), f32[1,1600,1024]{2,1,0:T(8,128)}) %all-reduce.15.cloned.1.call-update) | async-done | bytes 6553616 | tf_op jit(solution)/shard_map/psum | solution.py:222
  1626.4 5.1 multiply_reduce_fusion
  1632.9 22.0 %psum.52 = f32[]{:T(128)} all-reduce(f32[]{:T(128)} %multiply_reduce_fusion), channel_id=1, replica_groups=mesh['tile'=4,'dp'=8] {'dp'}, use_global_device_ids=true, to_apply=%region_18.19 | all-reduce | flops 1 | bytes 8 | tf_op jit(solution)/shard_map/psum | solution.py:227
  1657.7 0.7 multiply_subtract_fusion.1
  1658.4 0.6 multiply_subtract_fusion.2
  1659.0 17.3 %multiply_subtract_fusion = (f32[1,1600,1024]{2,1,0:T(8,128)}, f32[1,1600,1024]{2,1,0:T(8,128)}, f32[1,1600,1024]{2,1,0:T(8,128)}) fusion(f32[1,1600,1024]{2,1,0:T(8,128)} %param.24, f32[]{:T(128)} %bitcast.97, f32[1,1600,1024]{2,1,0:T(8,128)} %all-reduce.15.cloned.1.call-done, f32[]{:T(128)} %div.177, f32[1,1600,1024]{2,1,0:T(8,128)} %param.26, ...), kind=kLoop, calls=%fused_computation.10 | loop fusion | flops 24576000 | bytes 45875208 | tf_op jit(solution)/shard_map/sub | solution.py:130
  (249 shorter events, 11.2 us)
Async XLA Ops:
  7.2 509.5 %all-gather.3.cloned.1.call-start = ((), (), s32[]{:S(2)}) async-start(), calls=%async_computation.3 | async-start | bytes 29491200 | tf_op jit(solution)/shard_map/all_gather | solution.py:166
  12.3 0.7 copy-start.18
  12.3 0.7 copy-start.11
  12.3 0.9 copy-start.4
  12.3 5.9 copy-start.7
  12.3 5.9 copy-start.19
  12.4 1487.3 %reduce-scatter.2.cloned.1.call-start = ((), (), s32[]{:S(2)}) async-start(), calls=%async_computation.1 | async-start | bytes 58982400 | tf_op jit(solution)/shard_map/reduce_scatter | solution.py:221
  13.0 93.6 %copy-start.9 = (f32[2,32]{1,0:T(2,128)}, f32[2,32]{1,0:T(2,128)S(1)}, u32[]{:S(2)}) copy-start(f32[2,32]{1,0:T(2,128)S(1)} %get-tuple-element.135) | copy-start | bytes 772
  13.2 92.8 %collective-permute-start.1 = (bf16[1,2,32,512]{3,2,1,0:T(8,128)(2,1)S(1)}, bf16[1,2,32,512]{3,2,1,0:T(8,128)(2,1)S(1)}, u32[]{:S(2)}, u32[]{:S(2)}) collective-permute-start(bf16[1,2,32,512]{3,2,1,0:T(8,128)(2,1)S(1)} %pad_maximum_fusion.12), channel_id=1, source_target_pairs={{8,0},{16,8},{24,16},{9,1},{17,9},{25,17},{10,2},{18,10},{26,18},{... | collective-permute-start | bytes 196616 | tf_op jit(solution)/shard_map/ppermute | solution.py:23
  14.5 91.5 %collective-permute-start = (bf16[1,2,32,512]{3,2,1,0:T(8,128)(2,1)S(1)}, bf16[1,2,32,512]{3,2,1,0:T(8,128)(2,1)S(1)}, u32[]{:S(2)}, u32[]{:S(2)}) collective-permute-start(bf16[1,2,32,512]{3,2,1,0:T(8,128)(2,1)S(1)} %pad_maximum_fusion.12), channel_id=1, source_target_pairs={{0,8},{8,16},{16,24},{1,9},{9,17},{17,25},{2,10},{10,18},{18,26},{... | collective-permute-start | bytes 196616 | tf_op jit(solution)/shard_map/ppermute | solution.py:21
  107.0 1.2 copy-start.1
  528.8 1.2 copy-start.5
  530.1 56.6 %collective-permute-start.3 = (bf16[1,2,32,512]{3,2,1,0:T(8,128)(2,1)S(1)}, bf16[1,2,32,512]{3,2,1,0:T(8,128)(2,1)S(1)}, u32[]{:S(2)}, u32[]{:S(2)}) collective-permute-start(bf16[1,2,32,512]{3,2,1,0:T(8,128)(2,1)S(1)} %pad_maximum_fusion.13), channel_id=1, source_target_pairs={{8,0},{16,8},{24,16},{9,1},{17,9},{25,17},{10,2},{18,10},{26,18},{... | collective-permute-start | bytes 196616 | tf_op jit(solution)/shard_map/ppermute | solution.py:23
  531.4 55.3 %collective-permute-start.2 = (bf16[1,2,32,512]{3,2,1,0:T(8,128)(2,1)S(1)}, bf16[1,2,32,512]{3,2,1,0:T(8,128)(2,1)S(1)}, u32[]{:S(2)}, u32[]{:S(2)}) collective-permute-start(bf16[1,2,32,512]{3,2,1,0:T(8,128)(2,1)S(1)} %pad_maximum_fusion.13), channel_id=1, source_target_pairs={{0,8},{8,16},{16,24},{1,9},{9,17},{17,25},{2,10},{10,18},{18,26},{... | collective-permute-start | bytes 196616 | tf_op jit(solution)/shard_map/ppermute | solution.py:21
  587.6 1.2 copy-start
  601.1 1.8 copy-start.15
  602.8 41.9 %copy-start.3 = (f32[1,2,32,256]{3,2,1,0:T(8,128)}, f32[1,2,32,256]{3,2,1,0:T(8,128)S(1)}, u32[]{:S(2)}) copy-start(f32[1,2,32,256]{3,2,1,0:T(8,128)S(1)} %get-tuple-element.37) | copy-start | bytes 196612
  606.1 26.7 %collective-permute-start.5 = (bf16[1,2,32,1024]{3,2,1,0:T(8,128)(2,1)S(1)}, bf16[1,2,32,1024]{3,2,1,0:T(8,128)(2,1)S(1)}, u32[]{:S(2)}, u32[]{:S(2)}) collective-permute-start(bf16[1,2,32,1024]{3,2,1,0:T(8,128)(2,1)S(1)} %fusion.25), channel_id=1, source_target_pairs={{8,0},{16,8},{24,16},{9,1},{17,9},{25,17},{10,2},{18,10},{26,18},{... | collective-permute-start | bytes 393224 | tf_op jit(solution)/shard_map/ppermute | solution.py:23
  607.4 25.4 %collective-permute-start.4 = (bf16[1,2,32,1024]{3,2,1,0:T(8,128)(2,1)S(1)}, bf16[1,2,32,1024]{3,2,1,0:T(8,128)(2,1)S(1)}, u32[]{:S(2)}, u32[]{:S(2)}) collective-permute-start(bf16[1,2,32,1024]{3,2,1,0:T(8,128)(2,1)S(1)} %fusion.25), channel_id=1, source_target_pairs={{0,8},{8,16},{16,24},{1,9},{9,17},{17,25},{2,10},{10,18},{18,26},{... | collective-permute-start | bytes 393224 | tf_op jit(solution)/shard_map/ppermute | solution.py:21
  633.8 11.0 copy-start.6
  646.3 1.6 copy-start.2
  681.5 944.9 %all-reduce.15.cloned.1.call-start = ((), (), s32[]{:S(2)}) async-start(), calls=%async_computation.2 | async-start | bytes 13107200 | tf_op jit(solution)/shard_map/psum | solution.py:222
  683.5 9.1 collective-permute-start.7
  684.8 7.8 collective-permute-start.6
  1503.7 12.9 copy-start.10
  1560.0 97.7 %copy-start.8 = (f32[2,1,1024]{2,1,0:T(1,128)S(1)}, f32[2,1,1024]{2,1,0:T(1,128)}, u32[]{:S(2)}) copy-start(f32[2,1,1024]{2,1,0:T(1,128)} %param.27) | copy-start | bytes 24580
  1560.0 97.7 %copy-start.13 = (f32[2,1,1024]{2,1,0:T(1,128)S(1)}, f32[2,1,1024]{2,1,0:T(1,128)}, u32[]{:S(2)}) copy-start(f32[2,1,1024]{2,1,0:T(1,128)} %param.29) | copy-start | bytes 24580
  1560.0 97.7 %copy-start.14 = (f32[2,1,1024]{2,1,0:T(1,128)S(1)}, f32[2,1,1024]{2,1,0:T(1,128)}, u32[]{:S(2)}) copy-start(f32[2,1,1024]{2,1,0:T(1,128)} %param.28) | copy-start | bytes 24580
  1560.0 98.3 %copy-start.12 = (f32[3,256]{1,0:T(4,128)S(1)}, f32[3,256]{1,0:T(4,128)}, u32[]{:S(2)}) copy-start(f32[3,256]{1,0:T(4,128)} %param.30) | copy-start | bytes 9220
  1560.0 98.3 %copy-start.16 = (f32[3,256]{1,0:T(4,128)S(1)}, f32[3,256]{1,0:T(4,128)}, u32[]{:S(2)}) copy-start(f32[3,256]{1,0:T(4,128)} %param.32) | copy-start | bytes 9220
  1560.0 98.3 %copy-start.17 = (f32[3,256]{1,0:T(4,128)S(1)}, f32[3,256]{1,0:T(4,128)}, u32[]{:S(2)}) copy-start(f32[3,256]{1,0:T(4,128)} %param.31) | copy-start | bytes 9220
Sparse Core Ops, SparseCore 0:
  12.5 504.1 all-gather.2
  681.6 817.9 reduce-scatter.1
  1502.0 124.3 all-reduce.14
where the time goes:
time: 1690 us
  waiting for transfers between devices  1270 us (75%)
  blocking collectives  149 us (9%)
  matrix products  100 us (6%)
  local copies, waits for them, and re-layouts  76.5 us (5%)
  other arithmetic  41.9 us (2%)
  between operations  32.4 us (2%)
  starting transfers between devices  19.7 us (1%)
    reduce_scatter x1, waiting for transfers between devices, per_device(): lax.psum_scatter(grad_kernels, 'dp', scatter_dimension=1, tiled=True)  794 us
    all_gather x1, waiting for transfers between devices, per_device(): lax.all_gather(kernels[layer_no].astype(jnp.bfloat16), 'dp', axis=0, tile...  408 us
    psum x1, blocking collectives, per_device(): count = jnp.maximum(lax.psum(jnp.sum(valid), ('tile', 'dp')), 1.0)  85.6 us
    psum x1, waiting for transfers between devices, per_device(): shard = lax.psum(shard, 'tile')  66.4 us
    dot_general x2, matrix products, layer_backward(): lax.dot_general(unfold(padded, rows, columns), gates_low.reshape(-1, gate...  55.1 us
    transpose x2, local copies, waits for them, and re-layouts, layer_backward(): flipped.transpose(0, 1, 3, 2).reshape(KERNEL * KERNEL * gate_dim, in_dim)  52.3 us
    psum x1, blocking collectives, per_device(): lax.psum((grad_norms, grad_ends, grad_head, loss_sum), ('tile', 'dp'))  41.4 us
  transfers between devices with their start and end apart: 11, of which 3 were waited for; matrix products, arithmetic and copies ran while one was open for 6% of the time, Pallas kernels for 0%

commit v1 on v0

--- a/solution.py
+++ b/solution.py
@@ -219,7 +219,9 @@
     grad_ends = jnp.stack([grad_lift_weight, grad_lift_bias, grad_head_weight])
     grad_kernels = jnp.stack(kernel_grads)
     shard = lax.psum_scatter(grad_kernels, "dp", scatter_dimension=1, tiled=True)
-    shard = lax.psum(shard, "tile")
+    shard = shard
+    for hop in (1, 2):
+        shard = shard + lax.ppermute(shard, "tile", [(dev, dev ^ hop) for dev in range(4)])
     local_square = jnp.sum(shard * shard)
     grad_norms, grad_ends, grad_head, loss_sum = lax.psum(
         (grad_norms, grad_ends, grad_head, loss_sum), ("tile", "dp")

time: 1690 us -> 1770 us (1.047)
  blocking collectives: 149 us -> 271 us
  waiting for transfers between devices: 1270 us -> 1230 us
    psum x1, blocking collectives: 41.4 us -> 163 us  [per_device(): lax.psum((grad_norms, grad_ends, grad_head, loss_sum), ('tile', 'dp'))]
    psum x1 -> x0, waiting for transfers between devices: 66.4 us -> none  [per_device(): shard = lax.psum(shard, 'tile')]
    reduce_scatter x1, waiting for transfers between devices: 794 us -> 818 us  [per_device(): lax.psum_scatter(grad_kernels, 'dp', scatter_dimension=1, tiled=True)]
  transfers between devices with their start and end apart: 11 -> 12, of which waited for: 3 -> 3; matrix products, arithmetic and copies ran while one was open for 6% -> 5% of each run, Pallas kernels for 0% -> 0%
where the time goes in v1:
time: 1770 us
  waiting for transfers between devices  1230 us (69%)
  blocking collectives  271 us (15%)
  matrix products  98.3 us (6%)
  local copies, waits for them, and re-layouts  61.5 us (3%)
  other arithmetic  57.2 us (3%)
  between operations  32.9 us (2%)
  starting transfers between devices  19.9 us (1%)
    reduce_scatter x1, waiting for transfers between devices, per_device(): lax.psum_scatter(grad_kernels, 'dp', scatter_dimension=1, tiled=True)  818 us
    all_gather x1, waiting for transfers between devices, per_device(): lax.all_gather(kernels[layer_no].astype(jnp.bfloat16), 'dp', axis=0, tile...  408 us
    psum x1, blocking collectives, per_device(): lax.psum((grad_norms, grad_ends, grad_head, loss_sum), ('tile', 'dp'))  163 us
    psum x1, blocking collectives, per_device(): count = jnp.maximum(lax.psum(jnp.sum(valid), ('tile', 'dp')), 1.0)  85.6 us
    dot_general x2, matrix products, layer_backward(): lax.dot_general(unfold(padded, rows, columns), gates_low.reshape(-1, gate...  55.1 us
    transpose x2, local copies, waits for them, and re-layouts, layer_backward(): flipped.transpose(0, 1, 3, 2).reshape(KERNEL * KERNEL * gate_dim, in_dim)  52.3 us
  transfers between devices with their start and end apart: 12, of which 3 were waited for; matrix products, arithmetic and copies ran while one was open for 5% of the time, Pallas kernels for 0%

profile of v1, /device:TPU:0, one launch (start us, length us, event | category | flops | bytes accessed | tf_op | source)
XLA Modules:
  0.0 1767.7 jit_solution(3304890145225893677)
XLA Ops:
  7.2 5.1 convert_element_type.95
  12.4 0.6 copy-done.21
  13.2 1.3 collective-permute-start.1
  14.5 3.0 collective-permute-start
  18.2 0.7 fusion.79
  18.9 85.6 %psum.43 = f32[]{:T(128)} all-reduce(f32[]{:T(128)} %get-tuple-element.67), channel_id=1, replica_groups=mesh['tile'=4,'dp'=8] {'tile','dp'}, use_global_device_ids=true, to_apply=%region_10.11 | all-reduce | flops 1 | bytes 8 | tf_op jit(solution)/shard_map/psum | solution.py:159
  107.0 1.2 copy-done.1
  108.5 408.1 %all-gather.3.cloned.1.call-done = bf16[1,12800,1024]{2,1,0:T(8,128)(2,1)} async-done(((bf16[1,1600,1024]{2,1,0:T(8,128)(2,1)}), bf16[1,12800,1024]{2,1,0:T(8,128)(2,1)}) %all-gather.3.cloned.1.call-update) | async-done | bytes 26214416 | tf_op jit(solution)/shard_map/all_gather | solution.py:166
  516.7 10.8 fusion.3
  527.8 0.2 reduce_sum.247
  528.0 0.4 multiply_reduce_fusion.4
  528.4 0.2 mul.797
  528.6 0.2 mul.798
  528.8 0.2 sub.208
  529.0 0.2 sub.209
  529.2 0.8 multiply_add_fusion.2
  530.1 1.3 collective-permute-start.3
  531.4 3.0 collective-permute-start.2
  534.4 18.4 %reverse_bitcast_fusion = bf16[5,5,1024,512]{2,3,1,0:T(8,128)(2,1)} fusion(bf16[5,5,512,1024]{3,2,1,0:T(8,128)(2,1)} %bitcast.214), kind=kLoop, calls=%fused_computation.6 | loop fusion | bytes 52428800 | tf_op jit(solution)/shard_map/transpose | solution.py:93
  552.8 33.9 %copy.35 = bf16[5,5,1024,512]{3,2,1,0:T(8,128)(2,1)} copy(bf16[5,5,1024,512]{2,3,1,0:T(8,128)(2,1)} %reverse_bitcast_fusion) | data formatting | bytes 52428800 | tf_op jit(solution)/shard_map/transpose | solution.py:93
  588.0 0.7 copy-done
  588.8 10.8 fusion.1
  599.9 0.2 reduce_sum.254
  600.1 0.4 multiply_reduce_fusion.3
  600.5 0.2 mul.818
  600.7 0.2 mul.819
  600.9 0.2 sub.214
  601.3 0.8 multiply_add_fusion.1
  602.0 0.7 fusion.74
  602.9 0.6 fusion.67
  603.8 0.4 multiply_reduce_fusion.2
  604.2 0.6 fusion.20
  604.8 0.2 broadcast_in_dim.45
  605.2 0.2 broadcast_in_dim.20
  605.4 0.2 broadcast_in_dim.21
  605.6 1.0 fusion.25
  606.6 1.3 collective-permute-start.5
  607.9 3.8 collective-permute-start.4
  611.7 21.6 %fusion.11 = f32[12800,1024,1]{1,0,2:T(8,128)} fusion(bf16[1,2,32,12800]{3,2,1,0:T(8,128)(2,1)} %copy-done, bf16[1,2,32,1024]{3,2,1,0:T(8,128)(2,1)S(1)} %fusion.25), kind=kOutput, calls=%fused_computation.17 | convolution fusion | flops 1677721600 | bytes 54198272 | tf_op jit(solution)/shard_map/dot_general | solution.py:109
  634.4 10.8 fusion.13
  645.2 0.7 multiply_reduce_fusion.9
  646.2 0.4 multiply_reduce_fusion.1
  646.6 0.6 fusion.21
  647.3 0.2 broadcast_in_dim.50
  647.6 0.2 broadcast_in_dim.47
  647.8 0.2 broadcast_in_dim.48
  648.0 1.0 fusion.27
  649.1 33.5 %fusion = f32[1,12800,1024]{2,1,0:T(8,128)} fusion(f32[12800,1024,1]{1,0,2:T(8,128)} %fusion.11, bf16[1,2,32,12800]{3,2,1,0:T(8,128)(2,1)S(1)} %copy-done.2, bf16[1,2,32,1024]{3,2,1,0:T(8,128)(2,1)S(1)} %fusion.27), kind=kOutput, calls=%fused_computation.1 | convolution fusion | flops 1690828800 | bytes 106627072 | tf_op jit(solution)/shard_map/dot_general | solution.py:109
  682.6 818.0 %reduce-scatter.2.cloned.1.call-done = f32[1,1600,1024]{2,1,0:T(8,128)} async-done(((f32[1,12800,1024]{2,1,0:T(8,128)}), f32[1,1600,1024]{2,1,0:T(8,128)}) %reduce-scatter.2.cloned.1.call-update) | async-done | bytes 6553616 | tf_op jit(solution)/shard_map/reduce_scatter | solution.py:221
  1502.7 1.3 collective-permute-start.9
  1504.0 3.3 collective-permute-start.8
  1507.2 0.6 fusion.72
  1510.5 1.1 collective-permute-done.9
  1511.8 9.9 add.421
  1521.7 1.5 collective-permute-start.7
  1524.0 10.7 fusion.16
  1534.9 163.3 %all-reduce.12 = (f32[]{:T(128)}, f32[2,1,1024]{2,1,0:T(1,128)S(1)}, f32[3,256]{1,0:T(4,128)S(1)}, f32[1]{0:T(128)}) all-reduce(f32[]{:T(128)S(6)} %add.414, f32[2,1,1024]{2,1,0:T(1,128)S(1)} %pad_maximum_fusion.14, f32[3,256]{1,0:T(4,128)S(1)} %pad_maximum_fusion.15, f32[1]{0:T(128)} %bitcast.95), channel_id=1, replica_groups=mesh['tile'=4,'dp'=8] {'tile','dp'}, use_global_device_ids=true, to_apply=%region_8.9 | all-reduce | flops 2818 | bytes 22544 | tf_op jit(solution)/shard_map/psum | solution.py:226
  1700.1 0.6 multiply_reduce_fusion.14
  1700.7 0.6 multiply_reduce_fusion.13
  1701.4 10.7 multiply_reduce_fusion
  1712.0 21.7 %psum.44 = f32[]{:T(128)} all-reduce(f32[]{:T(128)} %get-tuple-element.47), channel_id=1, replica_groups=mesh['tile'=4,'dp'=8] {'dp'}, use_global_device_ids=true, to_apply=%region_17.18 | all-reduce | flops 1 | bytes 8 | tf_op jit(solution)/shard_map/psum | solution.py:229
  1736.6 0.7 multiply_subtract_fusion.1
  1737.3 0.6 multiply_subtract_fusion.2
  1737.9 17.3 multiply_subtract_fusion
  (257 shorter events, 6.2 us)
Async XLA Ops:
  7.2 509.5 %all-gather.3.cloned.1.call-start = ((), (), s32[]{:S(2)}) async-start(), calls=%async_computation.2 | async-start | bytes 29491200 | tf_op jit(solution)/shard_map/all_gather | solution.py:166
  12.3 0.7 copy-start.21
  12.3 0.7 copy-start.11
  12.3 0.9 copy-start.4
  12.3 5.9 copy-start.7
  12.3 5.9 copy-start.22
  12.4 1488.3 %reduce-scatter.2.cloned.1.call-start = ((), (), s32[]{:S(2)}) async-start(), calls=%async_computation.1 | async-start | bytes 58982400 | tf_op jit(solution)/shard_map/reduce_scatter | solution.py:221
  13.0 93.6 %copy-start.9 = (f32[2,32]{1,0:T(2,128)}, f32[2,32]{1,0:T(2,128)S(1)}, u32[]{:S(2)}) copy-start(f32[2,32]{1,0:T(2,128)S(1)} %get-tuple-element.137) | copy-start | bytes 772
  13.2 92.8 %collective-permute-start.1 = (bf16[1,2,32,512]{3,2,1,0:T(8,128)(2,1)S(1)}, bf16[1,2,32,512]{3,2,1,0:T(8,128)(2,1)S(1)}, u32[]{:S(2)}, u32[]{:S(2)}) collective-permute-start(bf16[1,2,32,512]{3,2,1,0:T(8,128)(2,1)S(1)} %pad_maximum_fusion.12), channel_id=1, source_target_pairs={{8,0},{16,8},{24,16},{9,1},{17,9},{25,17},{10,2},{18,10},{26,18},{... | collective-permute-start | bytes 196616 | tf_op jit(solution)/shard_map/ppermute | solution.py:23
  14.5 91.5 %collective-permute-start = (bf16[1,2,32,512]{3,2,1,0:T(8,128)(2,1)S(1)}, bf16[1,2,32,512]{3,2,1,0:T(8,128)(2,1)S(1)}, u32[]{:S(2)}, u32[]{:S(2)}) collective-permute-start(bf16[1,2,32,512]{3,2,1,0:T(8,128)(2,1)S(1)} %pad_maximum_fusion.12), channel_id=1, source_target_pairs={{0,8},{8,16},{16,24},{1,9},{9,17},{17,25},{2,10},{10,18},{18,26},{... | collective-permute-start | bytes 196616 | tf_op jit(solution)/shard_map/ppermute | solution.py:21
  107.0 1.2 copy-start.1
  528.8 1.2 copy-start.5
  530.1 56.6 %collective-permute-start.3 = (bf16[1,2,32,512]{3,2,1,0:T(8,128)(2,1)S(1)}, bf16[1,2,32,512]{3,2,1,0:T(8,128)(2,1)S(1)}, u32[]{:S(2)}, u32[]{:S(2)}) collective-permute-start(bf16[1,2,32,512]{3,2,1,0:T(8,128)(2,1)S(1)} %pad_maximum_fusion.13), channel_id=1, source_target_pairs={{8,0},{16,8},{24,16},{9,1},{17,9},{25,17},{10,2},{18,10},{26,18},{... | collective-permute-start | bytes 196616 | tf_op jit(solution)/shard_map/ppermute | solution.py:23
  531.4 55.3 %collective-permute-start.2 = (bf16[1,2,32,512]{3,2,1,0:T(8,128)(2,1)S(1)}, bf16[1,2,32,512]{3,2,1,0:T(8,128)(2,1)S(1)}, u32[]{:S(2)}, u32[]{:S(2)}) collective-permute-start(bf16[1,2,32,512]{3,2,1,0:T(8,128)(2,1)S(1)} %pad_maximum_fusion.13), channel_id=1, source_target_pairs={{0,8},{8,16},{16,24},{1,9},{9,17},{17,25},{2,10},{10,18},{18,26},{... | collective-permute-start | bytes 196616 | tf_op jit(solution)/shard_map/ppermute | solution.py:21
  587.6 1.2 copy-start
  601.1 1.8 copy-start.15
  602.8 42.4 %copy-start.3 = (f32[1,2,32,256]{3,2,1,0:T(8,128)}, f32[1,2,32,256]{3,2,1,0:T(8,128)S(1)}, u32[]{:S(2)}) copy-start(f32[1,2,32,256]{3,2,1,0:T(8,128)S(1)} %get-tuple-element.37) | copy-start | bytes 196612
  606.6 26.7 %collective-permute-start.5 = (bf16[1,2,32,1024]{3,2,1,0:T(8,128)(2,1)S(1)}, bf16[1,2,32,1024]{3,2,1,0:T(8,128)(2,1)S(1)}, u32[]{:S(2)}, u32[]{:S(2)}) collective-permute-start(bf16[1,2,32,1024]{3,2,1,0:T(8,128)(2,1)S(1)} %fusion.25), channel_id=1, source_target_pairs={{8,0},{16,8},{24,16},{9,1},{17,9},{25,17},{10,2},{18,10},{26,18},{... | collective-permute-start | bytes 393224 | tf_op jit(solution)/shard_map/ppermute | solution.py:23
  607.9 25.4 %collective-permute-start.4 = (bf16[1,2,32,1024]{3,2,1,0:T(8,128)(2,1)S(1)}, bf16[1,2,32,1024]{3,2,1,0:T(8,128)(2,1)S(1)}, u32[]{:S(2)}, u32[]{:S(2)}) collective-permute-start(bf16[1,2,32,1024]{3,2,1,0:T(8,128)(2,1)S(1)} %fusion.25), channel_id=1, source_target_pairs={{0,8},{8,16},{16,24},{1,9},{9,17},{17,25},{2,10},{10,18},{18,26},{... | collective-permute-start | bytes 393224 | tf_op jit(solution)/shard_map/ppermute | solution.py:21
  634.4 10.9 copy-start.16
  634.4 11.6 copy-start.6
  647.5 1.6 copy-start.2
  682.6 827.9 %copy-start.17 = (f32[256]{0:T(256)S(1)}, f32[256]{0:T(256)}, u32[]{:S(2)}) copy-start(f32[256]{0:T(256)} %get-tuple-element.124) | copy-start | bytes 3076
  682.6 827.9 %copy-start.18 = (f32[256]{0:T(256)S(1)}, f32[256]{0:T(256)}, u32[]{:S(2)}) copy-start(f32[256]{0:T(256)} %get-tuple-element.125) | copy-start | bytes 3076
  1500.7 11.2 collective-permute-start.6
  1502.7 8.9 collective-permute-start.9
  1504.0 7.6 collective-permute-start.8
  1521.7 179.6 %collective-permute-start.7 = (f32[1,1600,1024]{2,1,0:T(8,128)}, f32[1,1600,1024]{2,1,0:T(8,128)}, u32[]{:S(2)}, u32[]{:S(2)}) collective-permute-start(f32[1,1600,1024]{2,1,0:T(8,128)} %add.421), channel_id=1, source_target_pairs={{0,16},{8,24},{16,0},{24,8},{1,17},{9,25},{17,1},{25,9},{2,18},{10... | collective-permute-start | bytes 19660808 | tf_op jit(solution)/shard_map/ppermute | solution.py:224
  1524.0 10.8 copy-start.10
  1701.3 35.3 %copy-start.8 = (f32[2,1,1024]{2,1,0:T(1,128)S(1)}, f32[2,1,1024]{2,1,0:T(1,128)}, u32[]{:S(2)}) copy-start(f32[2,1,1024]{2,1,0:T(1,128)} %param.27) | copy-start | bytes 24580
  1701.3 35.3 %copy-start.13 = (f32[2,1,1024]{2,1,0:T(1,128)S(1)}, f32[2,1,1024]{2,1,0:T(1,128)}, u32[]{:S(2)}) copy-start(f32[2,1,1024]{2,1,0:T(1,128)} %param.29) | copy-start | bytes 24580
  1701.3 35.3 %copy-start.14 = (f32[2,1,1024]{2,1,0:T(1,128)S(1)}, f32[2,1,1024]{2,1,0:T(1,128)}, u32[]{:S(2)}) copy-start(f32[2,1,1024]{2,1,0:T(1,128)} %param.28) | copy-start | bytes 24580
  1701.3 36.0 %copy-start.12 = (f32[3,256]{1,0:T(4,128)S(1)}, f32[3,256]{1,0:T(4,128)}, u32[]{:S(2)}) copy-start(f32[3,256]{1,0:T(4,128)} %param.30) | copy-start | bytes 9220
  1701.3 36.0 %copy-start.19 = (f32[3,256]{1,0:T(4,128)S(1)}, f32[3,256]{1,0:T(4,128)}, u32[]{:S(2)}) copy-start(f32[3,256]{1,0:T(4,128)} %param.32) | copy-start | bytes 9220
  1701.3 36.0 %copy-start.20 = (f32[3,256]{1,0:T(4,128)S(1)}, f32[3,256]{1,0:T(4,128)}, u32[]{:S(2)}) copy-start(f32[3,256]{1,0:T(4,128)} %param.31) | copy-start | bytes 9220
Sparse Core Ops, SparseCore 0:
  12.5 504.1 all-gather.2
  682.7 817.8 reduce-scatter.1
